TPU v7x, 256 devices: a whole 4x4x8 slice. The times are simulated.
256 devices in a mesh: sec: 64 (over z, y, core), slab: 4 (over x).
Axes of the slice: x: 4, y: 4, z: 8, core: 2. Of those that a mesh axis runs over, the one named last changes fastest.
Arguments:
- basis: bfloat16 [128, 1024, 1024], P('sec'), may hold values from -0.1875 to 0.1875
- fermion: bfloat16 [3, 128, 1024, 1024], P(None, 'sec', None, 'slab'), may hold values from -6 to 6
- partner: int32 [3, 128], P(None, 'sec'), may hold values from 0 to 127, as said below
Outputs:
- rotated: bfloat16 [3, 128, 1024, 1024], P(None, 'sec', 'slab')
Inputs may be any that keep to these rules, and one draw needn't show every extreme that they name: partner[f, Q] // 2 equals Q // 2 or (Q // 2 + 1) % 64, so a partner lies in the block of 2 sectors that holds Q or in the next block, the last block's next being the first.
All inputs are finite; a program needn't handle non-finite values.
Results may differ from a plain program's by a relative error of at most 0.0049.
Values may be sent and summed in bfloat16 or wider, within the bound.
A program may use at most 64 MiB of HBM per device.

v0:
```python
import jax
import jax.numpy as jnp
from jax import lax
from jax.sharding import PartitionSpec as P


def shifted(block, axis, distance):
    devices = range(lax.axis_size(axis))
    route = [((i - distance) % len(devices), i) for i in devices]
    return lax.ppermute(block, axis, route)


def left_product(left_block, right_block):
    return lax.dot_general(
        left_block, right_block, (((0,), (0,)), ((), ())), preferred_element_type=jnp.float32
    ).astype(jnp.bfloat16)


def local(basis, fermion, partner):
    sectors_here = basis.shape[0]
    flavours = fermion.shape[0]
    all_sectors = sectors_here * lax.axis_size("sec")
    first_sector = lax.axis_index("sec") * sectors_here
    following = shifted(basis, "sec", -1)
    half_blocks = []
    for flavour in range(flavours):
        per_sector = []
        for sector in range(sectors_here):
            per_sector.append(left_product(basis[sector], fermion[flavour, sector]))
        half_blocks.append(jnp.stack(per_sector))
    half_rotated = jnp.stack(half_blocks)
    row_slabs = lax.all_to_all(half_rotated, "slab", split_axis=2, concat_axis=3, tiled=True)
    local_index = (partner - first_sector) % all_sectors
    out_blocks = []
    for flavour in range(flavours):
        per_sector = []
        for sector in range(sectors_here):
            where_index = local_index[flavour, sector]
            rows_here = row_slabs[flavour, sector]

            def from_own(operand):
                chosen = lax.dynamic_index_in_dim(
                    basis, jnp.minimum(where_index, sectors_here - 1), 0, keepdims=False
                )
                return jnp.dot(operand, chosen, preferred_element_type=jnp.float32)

            def from_next(operand):
                chosen = lax.dynamic_index_in_dim(
                    following, jnp.maximum(where_index - sectors_here, 0), 0, keepdims=False
                )
                return jnp.dot(operand, chosen, preferred_element_type=jnp.float32)

            product = lax.cond(where_index < sectors_here, from_own, from_next, rows_here)
            per_sector.append(product.astype(jnp.bfloat16))
        out_blocks.append(jnp.stack(per_sector))
    return jnp.stack(out_blocks)


def solution(mesh):
    placed = (P("sec", None, None), P(None, "sec", None, "slab"), P(None, "sec"))
    return jax.shard_map(
        local, mesh=mesh, in_specs=placed, out_specs=P(None, "sec", "slab", None), check_vma=False
    )
```

profile of v0, /device:TPU:88, one launch (start us, length us, event | category | flops | bytes accessed | tf_op | source)
XLA Modules:
  0.0 91.9 jit_solution(14583612871458534378)
XLA Ops:
  0.2 2.6 %fusion.159 = bf16[1,1024,256]{2,1,0:T(8,128)(2,1)S(1)} fusion(bf16[2,1024,1024]{2,1,0:T(8,128)(2,1)} %param.15, bf16[3,2,1024,256]{3,2,1,0:T(8,128)(2,1)} %param.16), kind=kOutput, calls=%fused_computation.99 | convolution fusion | flops 537133056 | bytes 3145728 | tf_op jit(solution)/shard_map/dot_general | solution.py:14
  3.0 1.0 %copy-done.6 = bf16[3,2,1024,256]{3,2,1,0:T(8,128)(2,1)S(1)} copy-done((bf16[3,2,1024,256]{3,2,1,0:T(8,128)(2,1)S(1)}, bf16[3,2,1024,256]{3,2,1,0:T(8,128)(2,1)}, u32[]{:S(2)}) %copy-start.6) | copy-done | bytes 3145752
  7.2 0.8 fusion.171
  8.5 4.9 %copy.11 = bf16[3,2,1024,256]{3,1,0,2:T(2,128)(2,1)} copy(bf16[3,2,1024,256]{3,2,1,0:T(8,128)(2,1)S(1)} %pad_maximum_fusion) | data formatting | bytes 6291456 | tf_op jit(solution)/shard_map/stack | solution.py:31
  13.4 4.4 %all-to-all-start = ((bf16[3,2,1024,256]{3,1,0,2:T(2,128)(2,1)}), bf16[3,2,1024,256]{3,1,0,2:T(2,128)(2,1)S(1)}, u32[]{:S(2)}, u32[]{:S(2)}) async-start(bf16[3,2,1024,256]{3,1,0,2:T(2,128)(2,1)} %copy.11), calls=%async_computation | async-start | bytes 6291456 | tf_op jit(solution)/shard_map/all_to_all | solution.py:32
  22.3 33.1 %all-to-all-done = bf16[3,2,1024,256]{3,1,0,2:T(2,128)(2,1)S(1)} async-done(((bf16[3,2,1024,256]{3,1,0,2:T(2,128)(2,1)}), bf16[3,2,1024,256]{3,1,0,2:T(2,128)(2,1)S(1)}, u32[]{:S(2)}, u32[]{:S(2)}) %all-to-all-start) | async-done | bytes 3145760 | tf_op jit(solution)/shard_map/all_to_all | solution.py:32
  55.4 4.1 %copy.12 = bf16[3,2,256,4,256]{4,3,2,1,0:T(4,128)(2,1)} copy(bf16[3,2,256,4,256]{4,1,0,2,3:T(2,128)(2,1)S(1)} %bitcast.245) | data formatting | bytes 6291456 | tf_op jit(solution)/shard_map/all_to_all | solution.py:32
  59.5 4.7 %all_to_all.16 = bf16[3,2,256,1024]{3,2,1,0:T(8,128)(2,1)S(1)} reshape(bf16[3,2,256,4,256]{4,3,2,1,0:T(4,128)(2,1)} %copy.12) | data formatting | bytes 6291456 | tf_op jit(solution)/shard_map/all_to_all | solution.py:32
  64.2 1.7 %slice_bitcast_fusion.5 = (bf16[256,1024]{1,0:T(8,128)(2,1)}, bf16[256,1024]{1,0:T(8,128)(2,1)}, bf16[256,1024]{1,0:T(8,128)(2,1)}, bf16[256,1024]{1,0:T(8,128)(...) fusion(bf16[3,2,256,1024]{3,2,1,0:T(8,128)(2,1)S(1)} %all_to_all.16), kind=kLoop, calls=%fused_computation.115 | loop fusion | bytes 6291456 | tf_op jit(solution)/shard_map/squeeze | solution.py:39
  65.9 3.3 %conditional.6 = (bf16[1,256,1024]{2,1,0:T(8,128)(2,1)S(1)}) conditional(s32[]{:T(128)} %convert_element_type.114, (s32[]{:T(128)}, bf16[2,1024,1024]{2,1,0:T(8,128)(2,1)}, bf16[256,1024]{1,0:T(8,128)(2,1)}) %tuple.53, (s32[]{:T(128)}, bf16[2,1024,1024]{2,1,0:T(8,128)(2,1)}, bf16[256,1024]{1,0:T(8,128)(2,1)}) %tuple.54), branch_computations={%region_0.1_spmd, %region_1.2_spmd} | conditional | flops 537133056 | bytes 4194362 | solution.py:53
  66.6 2.4 %fusion.6 = bf16[1,256,1024]{1,2,0:T(8,128)(2,1)S(1)} fusion(bf16[256,1024]{1,0:T(8,128)(2,1)} %get-tuple-element.103, bf16[2,1024,1024]{2,1,0:T(8,128)(2,1)} %get-tuple-element.101, s32[]{:T(128)S(6)} %max.12), kind=kOutput, calls=%fused_computation.4 | convolution fusion | flops 537133056 | bytes 3145732 | tf_op jit(solution)/shard_map/cond/branch_0_fun/dot_general | solution.py:51
  69.3 3.3 %conditional.7 = (bf16[1,256,1024]{2,1,0:T(8,128)(2,1)S(1)}) conditional(s32[]{:T(128)} %convert_element_type.121, (s32[]{:T(128)}, bf16[2,1024,1024]{2,1,0:T(8,128)(2,1)}, bf16[256,1024]{1,0:T(8,128)(2,1)S(1)}) %tuple.106, (s32[]{:T(128)}, bf16[2,1024,1024]{2,1,0:T(8,128)(2,1)}, bf16[256,1024]{1,0:T(8,128)(2,1)S(1)}) %tuple.107), branch_computations={%region_2.3_spmd, %region_3.4_spmd} | conditional | flops 537133056 | bytes 4194362 | solution.py:53
  70.0 2.4 %fusion.26 = bf16[1,256,1024]{1,2,0:T(8,128)(2,1)S(1)} fusion(bf16[256,1024]{1,0:T(8,128)(2,1)S(1)} %get-tuple-element.109, bf16[2,1024,1024]{2,1,0:T(8,128)(2,1)} %get-tuple-element.107, s32[]{:T(128)S(6)} %max.13), kind=kOutput, calls=%fused_computation.16 | convolution fusion | flops 537133056 | bytes 3145732 | tf_op jit(solution)/shard_map/cond/branch_0_fun/dot_general | solution.py:51
  72.7 3.3 %conditional.8 = (bf16[1,256,1024]{2,1,0:T(8,128)(2,1)S(1)}) conditional(s32[]{:T(128)} %convert_element_type.122, (s32[]{:T(128)}, bf16[2,1024,1024]{2,1,0:T(8,128)(2,1)}, bf16[256,1024]{1,0:T(8,128)(2,1)S(1)}) %tuple.104, (s32[]{:T(128)}, bf16[2,1024,1024]{2,1,0:T(8,128)(2,1)}, bf16[256,1024]{1,0:T(8,128)(2,1)S(1)}) %tuple.105), branch_computations={%region_4.5_spmd, %region_5.6_spmd} | conditional | flops 537133056 | bytes 4194362 | solution.py:53
  73.5 2.4 %fusion.56 = bf16[1,256,1024]{1,2,0:T(8,128)(2,1)S(1)} fusion(bf16[256,1024]{1,0:T(8,128)(2,1)S(1)} %get-tuple-element.118, bf16[2,1024,1024]{2,1,0:T(8,128)(2,1)} %get-tuple-element.116, s32[]{:T(128)S(6)} %select_n.27), kind=kOutput, calls=%fused_computation.34 | convolution fusion | flops 537133056 | bytes 3145732 | tf_op jit(solution)/shard_map/cond/branch_1_fun/dot_general | solution.py:45
  76.1 3.2 %conditional.9 = (bf16[1,256,1024]{2,1,0:T(8,128)(2,1)S(1)}) conditional(s32[]{:T(128)} %convert_element_type.123, (s32[]{:T(128)}, bf16[2,1024,1024]{2,1,0:T(8,128)(2,1)}, bf16[256,1024]{1,0:T(8,128)(2,1)S(1)}) %tuple.102, (s32[]{:T(128)}, bf16[2,1024,1024]{2,1,0:T(8,128)(2,1)}, bf16[256,1024]{1,0:T(8,128)(2,1)S(1)}) %tuple.103), branch_computations={%region_6.7_spmd, %region_7.8_spmd} | conditional | flops 537133056 | bytes 4194362 | solution.py:53
  76.6 2.4 %fusion.66 = bf16[1,256,1024]{1,2,0:T(8,128)(2,1)S(1)} fusion(bf16[256,1024]{1,0:T(8,128)(2,1)S(1)} %get-tuple-element.121, bf16[2,1024,1024]{2,1,0:T(8,128)(2,1)} %get-tuple-element.119, s32[]{:T(128)S(6)} %max.15), kind=kOutput, calls=%fused_computation.40 | convolution fusion | flops 537133056 | bytes 3145732 | tf_op jit(solution)/shard_map/cond/branch_0_fun/dot_general | solution.py:51
  79.3 5.4 %conditional.10 = (bf16[1,256,1024]{2,1,0:T(8,128)(2,1)S(1)}) conditional(s32[]{:T(128)} %convert_element_type.124, (s32[]{:T(128)}, bf16[2,1024,1024]{2,1,0:T(8,128)(2,1)}, bf16[256,1024]{1,0:T(8,128)(2,1)}) %tuple.61, (s32[]{:T(128)}, bf16[2,1024,1024]{2,1,0:T(8,128)(2,1)}, bf16[256,1024]{1,0:T(8,128)(2,1)}) %tuple.62), branch_computations={%region_8.9_spmd, %region_9.10_spmd} | conditional | flops 537133056 | bytes 4194362 | solution.py:53
  80.3 3.2 %fusion.96 = bf16[1,256,1024]{1,2,0:T(8,128)(2,1)} fusion(bf16[256,1024]{1,0:T(8,128)(2,1)} %get-tuple-element.130, bf16[2,1024,1024]{2,1,0:T(8,128)(2,1)} %get-tuple-element.128, s32[]{:T(128)S(6)} %select_n.29), kind=kOutput, calls=%fused_computation.58 | convolution fusion | flops 537133056 | bytes 3145732 | tf_op jit(solution)/shard_map/cond/branch_1_fun/dot_general | solution.py:45
  83.5 1.2 %copy.28 = bf16[1,256,1024]{2,1,0:T(8,128)(2,1)S(1)} copy(bf16[1,256,1024]{1,2,0:T(8,128)(2,1)} %fusion.96) | data formatting | bytes 1048576 | tf_op jit(solution)/shard_map/cond | solution.py:53
  84.8 5.0 %conditional.11 = (bf16[1,256,1024]{2,1,0:T(8,128)(2,1)S(1)}) conditional(s32[]{:T(128)} %convert_element_type.125, (s32[]{:T(128)}, bf16[2,1024,1024]{2,1,0:T(8,128)(2,1)}, bf16[256,1024]{1,0:T(8,128)(2,1)S(1)}) %tuple.100, (s32[]{:T(128)}, bf16[2,1024,1024]{2,1,0:T(8,128)(2,1)}, bf16[256,1024]{1,0:T(8,128)(2,1)S(1)}) %tuple.101), branch_computations={%region_10.11_spmd, %region_11.12_spmd} | conditional | flops 537133056 | bytes 4194362 | solution.py:53
  85.3 3.2 %fusion.106 = bf16[1,256,1024]{1,2,0:T(8,128)(2,1)} fusion(bf16[256,1024]{1,0:T(8,128)(2,1)S(1)} %get-tuple-element.133, bf16[2,1024,1024]{2,1,0:T(8,128)(2,1)} %get-tuple-element.131, s32[]{:T(128)S(6)} %max.17), kind=kOutput, calls=%fused_computation.64 | convolution fusion | flops 537133056 | bytes 3145732 | tf_op jit(solution)/shard_map/cond/branch_0_fun/dot_general | solution.py:51
  88.5 1.2 %copy.29 = bf16[1,256,1024]{2,1,0:T(8,128)(2,1)S(1)} copy(bf16[1,256,1024]{1,2,0:T(8,128)(2,1)} %fusion.106) | data formatting | bytes 1048576 | tf_op jit(solution)/shard_map/cond | solution.py:53
  89.9 2.0 %pad_maximum_fusion.1 = bf16[3,2,256,1024]{3,2,1,0:T(8,128)(2,1)} fusion(bf16[1,2,256,1024]{3,2,1,0:T(8,128)(2,1)S(1)} %maximum_bitcast_fusion.5, bf16[1,2,256,1024]{3,2,1,0:T(8,128)(2,1)S(1)} %maximum_bitcast_fusion.4, bf16[1,2,256,1024]{3,2,1,0:T(8,128)(2,1)S(1)} %maximum_bitcast_fusion.3), kind=kLoop, calls=%fused_computation.73 | loop fusion | flops 3145728 | bytes 6291456 | tf_op jit(solution)/shard_map/stack | solution.py:56
  (31 shorter events, 6.0 us)
Async XLA Ops:
  0.0 3.0 %copy-start.5 = (bf16[2,1024,1024]{2,1,0:T(8,128)(2,1)S(1)}, bf16[2,1024,1024]{2,1,0:T(8,128)(2,1)}, u32[]{:S(2)}) copy-start(bf16[2,1024,1024]{2,1,0:T(8,128)(2,1)} %param.15) | copy-start | bytes 12582916
  0.0 4.0 %copy-start.6 = (bf16[3,2,1024,256]{3,2,1,0:T(8,128)(2,1)S(1)}, bf16[3,2,1024,256]{3,2,1,0:T(8,128)(2,1)}, u32[]{:S(2)}) copy-start(bf16[3,2,1024,256]{3,2,1,0:T(8,128)(2,1)} %param.16) | copy-start | bytes 9437188
  0.0 65.9 %collective-permute-start = (bf16[2,1024,1024]{2,1,0:T(8,128)(2,1)}, bf16[2,1024,1024]{2,1,0:T(8,128)(2,1)}, u32[]{:S(2)}, u32[]{:S(2)}) collective-permute-start(bf16[2,1024,1024]{2,1,0:T(8,128)(2,1)} %param.15), channel_id=1, source_target_pairs={{4,0},{8,4},{12,8},{16,12},{20,16},{24,20},{28,24},{32,28},{36,32}... | collective-permute-start | bytes 12582920 | tf_op jit(solution)/shard_map/ppermute | solution.py:10
  13.4 4.4 %copy-start.4 = (s32[3,2]{0,1:T(2,128)S(1)}, s32[3,2]{0,1:T(2,128)}, u32[]{:S(2)}) copy-start(s32[3,2]{0,1:T(2,128)} %param.17) | copy-start | bytes 76
  13.4 42.0 %all-to-all-start = ((bf16[3,2,1024,256]{3,1,0,2:T(2,128)(2,1)}), bf16[3,2,1024,256]{3,1,0,2:T(2,128)(2,1)S(1)}, u32[]{:S(2)}, u32[]{:S(2)}) async-start(bf16[3,2,1024,256]{3,1,0,2:T(2,128)(2,1)} %copy.11), calls=%async_computation | async-start | bytes 6291456 | tf_op jit(solution)/shard_map/all_to_all | solution.py:32
  65.9 3.4 %copy-start.3 = (bf16[256,1024]{1,0:T(8,128)(2,1)S(1)}, bf16[256,1024]{1,0:T(8,128)(2,1)}, u32[]{:S(2)}) copy-start(bf16[256,1024]{1,0:T(8,128)(2,1)} %get-tuple-element.148) | copy-start | bytes 1572868
  69.3 3.4 %copy-start.2 = (bf16[256,1024]{1,0:T(8,128)(2,1)S(1)}, bf16[256,1024]{1,0:T(8,128)(2,1)}, u32[]{:S(2)}) copy-start(bf16[256,1024]{1,0:T(8,128)(2,1)} %get-tuple-element.147) | copy-start | bytes 1572868
  72.7 3.3 %copy-start.1 = (bf16[256,1024]{1,0:T(8,128)(2,1)S(1)}, bf16[256,1024]{1,0:T(8,128)(2,1)}, u32[]{:S(2)}) copy-start(bf16[256,1024]{1,0:T(8,128)(2,1)} %get-tuple-element.146) | copy-start | bytes 1572868
  79.3 5.4 %copy-start = (bf16[256,1024]{1,0:T(8,128)(2,1)S(1)}, bf16[256,1024]{1,0:T(8,128)(2,1)}, u32[]{:S(2)}) copy-start(bf16[256,1024]{1,0:T(8,128)(2,1)} %get-tuple-element.144) | copy-start | bytes 1572868
where the time goes:
time: 92.5 us; the launch traced here: 91.9 us
  waiting for transfers between devices  33.1 us (36%)
  matrix products  22.4 us (24%)
  local copies, waits for them, and re-layouts  20.6 us (22%)
  starting transfers between devices  4.61 us (5%)
  loops' own time  4.29 us (5%)
  between operations  3.95 us (4%)
  other arithmetic  2.94 us (3%)
    all_to_all x1, waiting for transfers between devices, local(): lax.all_to_all(half_rotated, 'slab', split_axis=2, concat_axis=3, tiled=T...  33.1 us
    dot_general x4, matrix products, from_next(): return jnp.dot(operand, chosen, preferred_element_type=jnp.float32)  10.3 us
    all_to_all x2, local copies, waits for them, and re-layouts, local(): lax.all_to_all(half_rotated, 'slab', split_axis=2, concat_axis=3, tiled=T...  8.77 us
    dot_general x6, matrix products, left_product(): lax.dot_general(left_block, right_block, (((0,), (0,)), ((), ())), prefer...  6.49 us
    dot_general x2, matrix products, from_own(): return jnp.dot(operand, chosen, preferred_element_type=jnp.float32)  5.59 us
    another operation x1, local copies, waits for them, and re-layouts, local(): half_rotated = jnp.stack(half_blocks)  4.9 us
    all_to_all x1, starting transfers between devices, local(): lax.all_to_all(half_rotated, 'slab', split_axis=2, concat_axis=3, tiled=T...  4.43 us
    another operation x6, loops' own time, local(): lax.cond(where_index < sectors_here, from_own, from_next, rows_here)  4.29 us
  transfers between devices with their start and end apart: 2, of which 1 were waited for; matrix products, arithmetic and copies ran while one was open for 20% of the time, Pallas kernels for 0%

commit v1 on v0

--- a/solution.py
+++ b/solution.py
@@ -29,7 +29,12 @@
             per_sector.append(left_product(basis[sector], fermion[flavour, sector]))
         half_blocks.append(jnp.stack(per_sector))
     half_rotated = jnp.stack(half_blocks)
-    row_slabs = lax.all_to_all(half_rotated, "slab", split_axis=2, concat_axis=3, tiled=True)
+    row_slabs = jnp.concatenate(
+        lax.all_to_all(
+            jnp.stack(jnp.split(half_rotated, lax.axis_size("slab"), axis=2)), "slab", 0, 0
+        ),
+        axis=3,
+    )
     local_index = (partner - first_sector) % all_sectors
     out_blocks = []
     for flavour in range(flavours):

time: 92.5 us -> 84.6 us (0.915)
  local copies, waits for them, and re-layouts: 20.6 us -> 11.2 us
  other arithmetic: 2.94 us -> 4.82 us
    all_to_all x2 -> x0, local copies, waits for them, and re-layouts: 8.77 us -> none  [local(): lax.all_to_all(half_rotated, 'slab', split_axis=2, concat_axis=3, tiled=T...]
    another operation x1, local copies, waits for them, and re-layouts: 4.9 us -> 0.21 us  [local(): jnp.stack(jnp.split(half_rotated, lax.axis_size('slab'), axis=2))]
    reshape x0 -> x1, local copies, waits for them, and re-layouts: none -> 2.76 us  [local(): jnp.concatenate(lax.all_to_all(jnp.stack(jnp.split(half_rotated, lax.axis...]
    another operation x0 -> x1, other arithmetic: none -> 1.88 us  [local(): jnp.stack(jnp.split(half_rotated, lax.axis_size('slab'), axis=2))]
    squeeze x1, local copies, waits for them, and re-layouts: 1.71 us -> 3.05 us  [local(): rows_here = row_slabs[flavour, sector]]
  transfers between devices with their start and end apart: 2 -> 2, of which waited for: 1 -> 1; matrix products, arithmetic and copies ran while one was open for 20% -> 19% of each run, Pallas kernels for 0% -> 0%
where the time goes in v1:
time: 84.6 us; the launch traced here: 84 us
  waiting for transfers between devices  33.2 us (39%)
  matrix products  22.3 us (26%)
  local copies, waits for them, and re-layouts  11.2 us (13%)
  other arithmetic  4.82 us (6%)
  starting transfers between devices  4.61 us (5%)
  loops' own time  4.04 us (5%)
  between operations  3.81 us (5%)
    all_to_all x1, waiting for transfers between devices, local(): lax.all_to_all(jnp.stack(jnp.split(half_rotated, lax.axis_size('slab'), a...  33.2 us
    dot_general x4, matrix products, from_next(): return jnp.dot(operand, chosen, preferred_element_type=jnp.float32)  10.2 us
    dot_general x6, matrix products, left_product(): lax.dot_general(left_block, right_block, (((0,), (0,)), ((), ())), prefer...  6.49 us
    dot_general x2, matrix products, from_own(): return jnp.dot(operand, chosen, preferred_element_type=jnp.float32)  5.59 us
    all_to_all x1, starting transfers between devices, local(): lax.all_to_all(jnp.stack(jnp.split(half_rotated, lax.axis_size('slab'), a...  4.42 us
    another operation x6, loops' own time, local(): lax.cond(where_index < sectors_here, from_own, from_next, rows_here)  4.04 us
    cond x6, local copies, waits for them, and re-layouts, local(): lax.cond(where_index < sectors_here, from_own, from_next, rows_here)  3.31 us
    squeeze x1, local copies, waits for them, and re-layouts, local(): rows_here = row_slabs[flavour, sector]  3.05 us
  transfers between devices with their start and end apart: 2, of which 1 were waited for; matrix products, arithmetic and copies ran while one was open for 19% of the time, Pallas kernels for 0%

profile of v1, /device:TPU:88, one launch (start us, length us, event | category | flops | bytes accessed | tf_op | source)
XLA Modules:
  0.0 84.0 jit_solution(8844779413349439218)
XLA Ops:
  0.2 2.6 %fusion.159 = bf16[1,1024,256]{2,1,0:T(8,128)(2,1)S(1)} fusion(bf16[2,1024,1024]{2,1,0:T(8,128)(2,1)} %param.15, bf16[3,2,1024,256]{3,2,1,0:T(8,128)(2,1)} %param.16), kind=kOutput, calls=%fused_computation.100 | convolution fusion | flops 537133056 | bytes 3145728 | tf_op jit(solution)/shard_map/dot_general | solution.py:14
  3.0 1.0 %copy-done.3 = bf16[3,2,1024,256]{3,2,1,0:T(8,128)(2,1)S(1)} copy-done((bf16[3,2,1024,256]{3,2,1,0:T(8,128)(2,1)S(1)}, bf16[3,2,1024,256]{3,2,1,0:T(8,128)(2,1)}, u32[]{:S(2)}) %copy-start.3) | copy-done | bytes 3145752
  5.5 0.8 fusion.156
  6.3 0.8 fusion.165
  8.8 1.9 %pad_maximum_fusion.1 = bf16[4,3,2,256,256]{4,3,2,1,0:T(8,128)(2,1)} fusion(bf16[1,3,2,256,256]{4,3,2,1,0:T(8,128)(2,1)S(1)} %get-tuple-element.186, bf16[1,3,2,256,256]{4,3,2,1,0:T(8,128)(2,1)S(1)} %get-tuple-element.187, bf16[1,3,2,256,256]{4,3,2,1,0:T(8,128)(2,1)S(1)} %get-tuple-element.188, bf16[1,3,2,256,256]{4,3,2,1,0:T(8,128)(2,1)S(1)} %get-tuple-element.185), kind=kLoop, calls=%fused_computation.73 | loop fusion | flops 4718592 | bytes 6291456 | tf_op jit(solution)/shard_map/stack | solution.py:34
  10.6 4.4 %all-to-all-start = ((bf16[4,3,2,256,256]{4,3,2,1,0:T(8,128)(2,1)}), bf16[4,3,2,256,256]{4,3,2,1,0:T(8,128)(2,1)S(1)}, u32[]{:S(2)}, u32[]{:S(2)}) async-start(bf16[4,3,2,256,256]{4,3,2,1,0:T(8,128)(2,1)} %pad_maximum_fusion.1), calls=%async_computation | async-start | bytes 6291456 | tf_op jit(solution)/shard_map/all_to_all | solution.py:33
  19.4 33.2 %all-to-all-done = bf16[4,3,2,256,256]{4,3,2,1,0:T(8,128)(2,1)S(1)} async-done(((bf16[4,3,2,256,256]{4,3,2,1,0:T(8,128)(2,1)}), bf16[4,3,2,256,256]{4,3,2,1,0:T(8,128)(2,1)S(1)}, u32[]{:S(2)}, u32[]{:S(2)}) %all-to-all-start) | async-done | bytes 3145760 | tf_op jit(solution)/shard_map/all_to_all | solution.py:33
  52.6 2.8 %copy.10 = bf16[3,2,256,4,256]{2,4,3,1,0:T(8,128)(2,1)} copy(bf16[3,2,256,4,256]{4,2,1,0,3:T(8,128)(2,1)S(1)} %bitcast.252) | data formatting | bytes 6291456 | tf_op jit(solution)/shard_map/reshape | solution.py:32
  55.4 3.0 %slice_bitcast_fusion.9 = (bf16[256,1024]{0,1:T(8,128)(2,1)S(1)}, bf16[256,1024]{0,1:T(8,128)(2,1)}, bf16[256,1024]{0,1:T(8,128)(2,1)}, bf16[256,1024]{0,1:T(8,1...) fusion(bf16[3,2,256,1024]{2,3,1,0:T(8,128)(2,1)} %bitcast.253), kind=kLoop, calls=%fused_computation.120 | loop fusion | bytes 6291456 | tf_op jit(solution)/shard_map/squeeze | solution.py:44
  58.4 3.1 %conditional.6 = (bf16[1,256,1024]{2,1,0:T(8,128)(2,1)S(1)}) conditional(s32[]{:T(128)} %convert_element_type.114, (s32[]{:T(128)}, bf16[2,1024,1024]{2,1,0:T(8,128)(2,1)}, bf16[256,1024]{0,1:T(8,128)(2,1)S(1)}) %tuple.53, (s32[]{:T(128)}, bf16[2,1024,1024]{2,1,0:T(8,128)(2,1)}, bf16[256,1024]{0,1:T(8,128)(2,1)S(1)}) %tuple.54), branch_computations={%region_0.1_spmd, %region_1.2_spmd} | conditional | flops 537133056 | bytes 4194362 | solution.py:58
  59.0 2.4 %fusion.6 = bf16[1,256,1024]{1,2,0:T(8,128)(2,1)S(1)} fusion(bf16[256,1024]{0,1:T(8,128)(2,1)S(1)} %get-tuple-element.139, bf16[2,1024,1024]{2,1,0:T(8,128)(2,1)} %get-tuple-element.101, s32[]{:T(128)S(6)} %max.12), kind=kOutput, calls=%fused_computation.4 | convolution fusion | flops 537133056 | bytes 3145732 | tf_op jit(solution)/shard_map/cond/branch_0_fun/dot_general | solution.py:56
  61.6 3.2 %conditional.7 = (bf16[1,256,1024]{2,1,0:T(8,128)(2,1)S(1)}) conditional(s32[]{:T(128)} %convert_element_type.121, (s32[]{:T(128)}, bf16[2,1024,1024]{2,1,0:T(8,128)(2,1)}, bf16[256,1024]{0,1:T(8,128)(2,1)S(1)}) %tuple.55, (s32[]{:T(128)}, bf16[2,1024,1024]{2,1,0:T(8,128)(2,1)}, bf16[256,1024]{0,1:T(8,128)(2,1)S(1)}) %tuple.56), branch_computations={%region_2.3_spmd, %region_3.4_spmd} | conditional | flops 537133056 | bytes 4194362 | solution.py:58
  62.2 2.4 %fusion.26 = bf16[1,256,1024]{1,2,0:T(8,128)(2,1)S(1)} fusion(bf16[256,1024]{0,1:T(8,128)(2,1)S(1)} %get-tuple-element.145, bf16[2,1024,1024]{2,1,0:T(8,128)(2,1)} %get-tuple-element.107, s32[]{:T(128)S(6)} %max.13), kind=kOutput, calls=%fused_computation.16 | convolution fusion | flops 537133056 | bytes 3145732 | tf_op jit(solution)/shard_map/cond/branch_0_fun/dot_general | solution.py:56
  64.9 3.3 %conditional.8 = (bf16[1,256,1024]{2,1,0:T(8,128)(2,1)S(1)}) conditional(s32[]{:T(128)} %convert_element_type.122, (s32[]{:T(128)}, bf16[2,1024,1024]{2,1,0:T(8,128)(2,1)}, bf16[256,1024]{0,1:T(8,128)(2,1)S(1)}) %tuple.57, (s32[]{:T(128)}, bf16[2,1024,1024]{2,1,0:T(8,128)(2,1)}, bf16[256,1024]{0,1:T(8,128)(2,1)S(1)}) %tuple.58), branch_computations={%region_4.5_spmd, %region_5.6_spmd} | conditional | flops 537133056 | bytes 4194362 | solution.py:58
  65.7 2.4 %fusion.56 = bf16[1,256,1024]{1,2,0:T(8,128)(2,1)S(1)} fusion(bf16[256,1024]{0,1:T(8,128)(2,1)S(1)} %get-tuple-element.154, bf16[2,1024,1024]{2,1,0:T(8,128)(2,1)} %get-tuple-element.116, s32[]{:T(128)S(6)} %select_n.27), kind=kOutput, calls=%fused_computation.34 | convolution fusion | flops 537133056 | bytes 3145732 | tf_op jit(solution)/shard_map/cond/branch_1_fun/dot_general | solution.py:50
  68.3 3.2 %conditional.9 = (bf16[1,256,1024]{2,1,0:T(8,128)(2,1)S(1)}) conditional(s32[]{:T(128)} %convert_element_type.123, (s32[]{:T(128)}, bf16[2,1024,1024]{2,1,0:T(8,128)(2,1)}, bf16[256,1024]{0,1:T(8,128)(2,1)S(1)}) %tuple.59, (s32[]{:T(128)}, bf16[2,1024,1024]{2,1,0:T(8,128)(2,1)}, bf16[256,1024]{0,1:T(8,128)(2,1)S(1)}) %tuple.60), branch_computations={%region_6.7_spmd, %region_7.8_spmd} | conditional | flops 537133056 | bytes 4194362 | solution.py:58
  68.9 2.4 %fusion.66 = bf16[1,256,1024]{1,2,0:T(8,128)(2,1)S(1)} fusion(bf16[256,1024]{0,1:T(8,128)(2,1)S(1)} %get-tuple-element.157, bf16[2,1024,1024]{2,1,0:T(8,128)(2,1)} %get-tuple-element.119, s32[]{:T(128)S(6)} %max.15), kind=kOutput, calls=%fused_computation.40 | convolution fusion | flops 537133056 | bytes 3145732 | tf_op jit(solution)/shard_map/cond/branch_0_fun/dot_general | solution.py:56
  71.6 5.2 %conditional.10 = (bf16[1,256,1024]{2,1,0:T(8,128)(2,1)S(1)}) conditional(s32[]{:T(128)} %convert_element_type.124, (s32[]{:T(128)}, bf16[2,1024,1024]{2,1,0:T(8,128)(2,1)}, bf16[256,1024]{0,1:T(8,128)(2,1)}) %tuple.61, (s32[]{:T(128)}, bf16[2,1024,1024]{2,1,0:T(8,128)(2,1)}, bf16[256,1024]{0,1:T(8,128)(2,1)}) %tuple.62), branch_computations={%region_8.9_spmd, %region_9.10_spmd} | conditional | flops 537133056 | bytes 4194362 | solution.py:58
  72.3 3.2 %fusion.96 = bf16[1,256,1024]{1,2,0:T(8,128)(2,1)} fusion(bf16[256,1024]{0,1:T(8,128)(2,1)} %get-tuple-element.166, bf16[2,1024,1024]{2,1,0:T(8,128)(2,1)} %get-tuple-element.128, s32[]{:T(128)S(6)} %select_n.29), kind=kOutput, calls=%fused_computation.58 | convolution fusion | flops 537133056 | bytes 3145732 | tf_op jit(solution)/shard_map/cond/branch_1_fun/dot_general | solution.py:50
  75.5 1.2 %copy.50 = bf16[1,256,1024]{2,1,0:T(8,128)(2,1)S(1)} copy(bf16[1,256,1024]{1,2,0:T(8,128)(2,1)} %fusion.96) | data formatting | bytes 1048576 | tf_op jit(solution)/shard_map/cond | solution.py:58
  76.8 5.1 %conditional.11 = (bf16[1,256,1024]{2,1,0:T(8,128)(2,1)S(1)}) conditional(s32[]{:T(128)} %convert_element_type.125, (s32[]{:T(128)}, bf16[2,1024,1024]{2,1,0:T(8,128)(2,1)}, bf16[256,1024]{0,1:T(8,128)(2,1)S(1)}) %tuple.115, (s32[]{:T(128)}, bf16[2,1024,1024]{2,1,0:T(8,128)(2,1)}, bf16[256,1024]{0,1:T(8,128)(2,1)S(1)}) %tuple.116), branch_computations={%region_10.11_spmd, %region_11.12_spmd} | conditional | flops 537133056 | bytes 4194362 | solution.py:58
  77.5 3.2 %fusion.106 = bf16[1,256,1024]{1,2,0:T(8,128)(2,1)} fusion(bf16[256,1024]{0,1:T(8,128)(2,1)S(1)} %get-tuple-element.169, bf16[2,1024,1024]{2,1,0:T(8,128)(2,1)} %get-tuple-element.131, s32[]{:T(128)S(6)} %max.17), kind=kOutput, calls=%fused_computation.64 | convolution fusion | flops 537133056 | bytes 3145732 | tf_op jit(solution)/shard_map/cond/branch_0_fun/dot_general | solution.py:56
  80.6 1.2 %copy.51 = bf16[1,256,1024]{2,1,0:T(8,128)(2,1)S(1)} copy(bf16[1,256,1024]{1,2,0:T(8,128)(2,1)} %fusion.106) | data formatting | bytes 1048576 | tf_op jit(solution)/shard_map/cond | solution.py:58
  82.0 2.0 %pad_maximum_fusion.2 = bf16[3,2,256,1024]{3,2,1,0:T(8,128)(2,1)} fusion(bf16[1,2,256,1024]{3,2,1,0:T(8,128)(2,1)S(1)} %maximum_bitcast_fusion.5, bf16[1,2,256,1024]{3,2,1,0:T(8,128)(2,1)S(1)} %maximum_bitcast_fusion.4, bf16[1,2,256,1024]{3,2,1,0:T(8,128)(2,1)S(1)} %maximum_bitcast_fusion.3), kind=kLoop, calls=%fused_computation.74 | loop fusion | flops 3145728 | bytes 6291456 | tf_op jit(solution)/shard_map/stack | solution.py:61
  (25 shorter events, 5.4 us)
Async XLA Ops:
  0.0 3.0 %copy-start.2 = (bf16[2,1024,1024]{2,1,0:T(8,128)(2,1)S(1)}, bf16[2,1024,1024]{2,1,0:T(8,128)(2,1)}, u32[]{:S(2)}) copy-start(bf16[2,1024,1024]{2,1,0:T(8,128)(2,1)} %param.15) | copy-start | bytes 12582916
  0.0 4.0 %copy-start.3 = (bf16[3,2,1024,256]{3,2,1,0:T(8,128)(2,1)S(1)}, bf16[3,2,1024,256]{3,2,1,0:T(8,128)(2,1)}, u32[]{:S(2)}) copy-start(bf16[3,2,1024,256]{3,2,1,0:T(8,128)(2,1)} %param.16) | copy-start | bytes 9437188
  0.0 58.4 %collective-permute-start = (bf16[2,1024,1024]{2,1,0:T(8,128)(2,1)}, bf16[2,1024,1024]{2,1,0:T(8,128)(2,1)}, u32[]{:S(2)}, u32[]{:S(2)}) collective-permute-start(bf16[2,1024,1024]{2,1,0:T(8,128)(2,1)} %param.15), channel_id=1, source_target_pairs={{4,0},{8,4},{12,8},{16,12},{20,16},{24,20},{28,24},{32,28},{36,32}... | collective-permute-start | bytes 12582920 | tf_op jit(solution)/shard_map/ppermute | solution.py:10
  10.6 4.4 %copy-start.1 = (s32[3,2]{0,1:T(2,128)S(1)}, s32[3,2]{0,1:T(2,128)}, u32[]{:S(2)}) copy-start(s32[3,2]{0,1:T(2,128)} %param.17) | copy-start | bytes 76
  10.6 42.0 %all-to-all-start = ((bf16[4,3,2,256,256]{4,3,2,1,0:T(8,128)(2,1)}), bf16[4,3,2,256,256]{4,3,2,1,0:T(8,128)(2,1)S(1)}, u32[]{:S(2)}, u32[]{:S(2)}) async-start(bf16[4,3,2,256,256]{4,3,2,1,0:T(8,128)(2,1)} %pad_maximum_fusion.1), calls=%async_computation | async-start | bytes 6291456 | tf_op jit(solution)/shard_map/all_to_all | solution.py:33
  71.6 5.2 %copy-start = (bf16[256,1024]{0,1:T(8,128)(2,1)S(1)}, bf16[256,1024]{0,1:T(8,128)(2,1)}, u32[]{:S(2)}) copy-start(bf16[256,1024]{0,1:T(8,128)(2,1)} %get-tuple-element.180) | copy-start | bytes 1572868
